TPU v7x, 32 devices: a whole 2x2x4 slice. The times are simulated.
32 devices in a mesh: ex: 4 (over z), col: 4 (over y, core), lay: 2 (over x).
Axes of the slice: x: 2, y: 2, z: 4, core: 2. Of those that a mesh axis runs over, the one named last changes fastest.
Arguments:
- normalized: bfloat16 [256, 2, 4, 3584], P('ex', 'lay', None, 'col'), may hold values from -6 to 6
- upstream: bfloat16 [256, 2, 4, 3584], P('ex', 'lay', None, 'col'), may hold values from -3 to 3
- owner_order: int32 [4, 64], P('ex'), may hold values from 0 to 63, each once within a row
- sketch_index: int32 [2, 28, 4], P(None, 'col'), may hold values from 0 to 63, all different within a row
- sketch_scale: bfloat16 [2, 28, 4], P(None, 'col'), may hold values from -1.5 to 1.5
- query_sketch: bfloat16 [4, 8192], P('ex', 'col'), may hold values from -0.0625 to 0.0625
Outputs:
- sketch: bfloat16 [256, 8192], P(('ex', 'lay'), 'col')
- scores: float32 [256, 4], P(('ex', 'lay'), 'col')
Inputs may be any that keep to these rules, and one draw needn't show every extreme that they name: Each row is an ordering of the 64 examples of one block; the example at place j of row g is training example g * 64 + owner_order[g, j]. `sketch_index`: the 4 output blocks of one input block are distinct; every output block is named by some input block.
All inputs are finite; a program needn't handle non-finite values.
Results may differ from a plain program's by a relative error of at most 0.0049.
Values may be sent and summed in bfloat16 or wider, within the bound.
A program may use at most 64 MiB of HBM per device.

v0:
```python
import math
import jax
import jax.numpy as jnp
from jax import lax
from jax.sharding import PartitionSpec as P

SKETCH = 8192


def hadamard_table():
    counter = jnp.arange(128, dtype=jnp.int32)
    both = counter[:, None] & counter[None, :]
    parity = jnp.zeros((128, 128), jnp.int32)
    for shift_bit in range(7):
        parity = parity + (both >> shift_bit & 1)
    signs = 1 - 2 * (parity % 2)
    return signs.astype(jnp.float32) / math.sqrt(128.0)


def build_table(sketch_index, sketch_scale, out_blocks):
    targets = jnp.arange(out_blocks, dtype=jnp.int32)
    table = (sketch_index[..., None] == targets).astype(jnp.float32) * sketch_scale.astype(
        jnp.float32
    )[..., None]
    return jnp.sum(table, axis=2).reshape(-1, out_blocks)


def local(normalized, upstream, owner_order, sketch_index, sketch_scale, query_sketch):
    local_grads = jnp.sum(
        normalized.astype(jnp.float32) * upstream.astype(jnp.float32), axis=2
    ).astype(jnp.bfloat16)
    reordered = jnp.take(local_grads, owner_order[0], axis=0)
    owned = lax.all_to_all(reordered, "lay", split_axis=0, concat_axis=1, tiled=True)
    own_rows = owned.shape[0]
    out_blocks = SKETCH // 128
    full_rows, full_index, full_scale = (
        lax.all_gather(owned, "col", axis=2, tiled=True),
        lax.all_gather(sketch_index, "col", axis=1, tiled=True),
        lax.all_gather(sketch_scale, "col", axis=1, tiled=True),
    )
    layer_count, feature_width = (full_rows.shape[1], full_rows.shape[2])
    table = build_table(full_index, full_scale, out_blocks)
    my_blocks = out_blocks // lax.axis_size("col")
    my_table = lax.dynamic_slice_in_dim(table, lax.axis_index("col") * my_blocks, my_blocks, 1)
    grad_rows = full_rows.reshape(own_rows, layer_count * (feature_width // 128), 128).astype(
        jnp.float32
    )
    summed = jnp.einsum("ebc,bo->eoc", grad_rows, my_table, precision=lax.Precision.HIGHEST)
    rotated = jnp.einsum("eoc,cd->eod", summed, hadamard_table(), precision=lax.Precision.HIGHEST)
    sketch = rotated.reshape(own_rows, -1).astype(jnp.bfloat16)
    partial_scores = jnp.einsum(
        "ec,qc->eq",
        sketch,
        lax.all_gather(query_sketch, "ex", axis=0, tiled=True),
        preferred_element_type=jnp.float32,
    )
    scores = lax.psum_scatter(partial_scores, "col", scatter_dimension=1, tiled=True)
    return (sketch, scores)


def solution(mesh):
    placed = (
        P("ex", "lay", None, "col"),
        P("ex", "lay", None, "col"),
        P("ex", None),
        P(None, "col", None),
        P(None, "col", None),
        P("ex", "col"),
    )
    return jax.shard_map(
        local,
        mesh=mesh,
        in_specs=placed,
        out_specs=(P(("ex", "lay"), "col"), P(("ex", "lay"), "col")),
        check_vma=False,
    )
```

profile of v0, /device:TPU:0, one launch (start us, length us, event | category | flops | bytes accessed | tf_op | source)
XLA Modules:
  0.0 53.9 jit_solution(2970445033246631568)
XLA Ops:
  0.6 0.0 copy-start.4
  0.6 0.7 %fusion.23 = s32[64]{0:T(128)S(1)} fusion(s32[1,64]{1,0:T(1,128)} %param.8), kind=kLoop, calls=%fused_computation.37 | loop fusion | flops 192 | bytes 512 | tf_op jit(solution)/shard_map/jit(_take)/jit(_where)/select_n | solution.py:32
  1.4 0.0 copy-done.4
  1.4 1.8 %multiply_reduce_fusion = bf16[64,896]{1,0:T(8,128)(2,1)S(1)} fusion(bf16[64,1,4,896]{3,2,1,0:T(4,128)(2,1)} %param.7, bf16[64,1,4,896]{3,2,1,0:T(4,128)(2,1)} %param.6), kind=kLoop, calls=%fused_computation.3 | loop fusion | flops 860160 | bytes 1032192 | tf_op jit(solution)/shard_map/reduce_sum | solution.py:29
  3.2 0.7 %gather_fusion = bf16[64,896]{1,0:T(8,128)(2,1)S(1)} fusion(bf16[64,896]{1,0:T(8,128)(2,1)S(1)} %multiply_reduce_fusion, s32[1024]{0:T(1024)S(1)} %pad_clamp_fusion), kind=kCustom, calls=%fused_computation | custom fusion | bytes 229632 | tf_op jit(solution)/shard_map/jit(_take)/gather | solution.py:32
  3.9 0.1 bitcast_select_fusion
  4.0 0.5 broadcast.80
  4.6 0.7 %reduce.1 = bf16[64,896]{1,0:T(8,128)(2,1)S(1)} reduce(bf16[64,1,896]{2,0,1:T(8,128)(2,1)S(1)} %bitcast_select_fusion, bf16[]{:T(256)} %broadcast.80), dimensions={1}, to_apply=%copy.40.reduce_sub_computation | reduce | bytes 229378 | tf_op jit(solution)/shard_map/jit(_take)/select_n | solution.py:32
  5.2 0.7 %reshape.102 = bf16[2,2,14336]{2,1,0:T(2,128)(2,1)} reshape(bf16[64,896]{1,0:T(8,128)(2,1)S(1)} %reduce.1) | data formatting | bytes 229376
  5.9 0.0 copy-start.3
  5.9 4.4 %all-to-all-start = ((bf16[2,2,14336]{2,1,0:T(2,128)(2,1)}), bf16[2,2,14336]{2,1,0:T(2,128)(2,1)S(1)}, u32[]{:S(2)}, u32[]{:S(2)}) async-start(bf16[2,2,14336]{2,1,0:T(2,128)(2,1)} %reshape.102), calls=%async_computation | async-start | bytes 229376 | tf_op jit(solution)/shard_map/all_to_all | solution.py:33
  10.3 0.0 copy-done.3
  10.3 0.1 copy.36
  10.4 5.4 %all_gather.13 = bf16[2,28,4]{2,0,1:T(2,128)(2,1)S(1)} all-gather(bf16[2,7,4]{2,0,1:T(2,128)(2,1)S(1)} %copy.36), channel_id=1, replica_groups=mesh['ex'=4,'col'=4,'lay'=2] {'col'}, dimensions={1}, use_global_device_ids=true | all-gather | bytes 560 | tf_op jit(solution)/shard_map/all_gather | solution.py:39
  15.8 0.1 copy.37
  15.9 0.0 copy-start.2
  15.9 0.1 copy.38
  16.0 0.6 %copy-done.2 = s32[2,7,4]{1,2,0:T(4,128)S(1)} copy-done((s32[2,7,4]{1,2,0:T(4,128)S(1)}, s32[2,7,4]{1,2,0:T(4,128)}, u32[]{:S(2)}) %copy-start.2) | copy-done | bytes 248
  16.6 0.1 copy.34
  16.7 5.4 %all_gather.12 = s32[2,28,4]{2,0,1:T(2,128)S(1)} all-gather(s32[2,7,4]{2,0,1:T(2,128)S(1)} %copy.34), channel_id=1, replica_groups=mesh['ex'=4,'col'=4,'lay'=2] {'col'}, dimensions={1}, use_global_device_ids=true | all-gather | bytes 1120 | tf_op jit(solution)/shard_map/all_gather | solution.py:38
  22.1 0.2 select_reduce_fusion
  22.3 0.0 copy-start.1
  22.4 0.0 copy-start.5
  22.4 0.6 %copy-done.5 = u32[32]{0:T(128)S(1)} copy-done((u32[32]{0:T(128)S(1)}, u32[32]{0:T(128)}, u32[]{:S(2)}) %copy-start.5) | copy-done | bytes 152
  23.0 0.7 %dynamic-slice = u32[1]{0:T(128)} dynamic-slice(u32[32]{0:T(128)S(1)} %copy-done.5, u32[]{:T(128)S(6)} %add.63), dynamic_slice_sizes={1} | dynamic-slice | bytes 12
  23.7 0.0 copy-done.1
  23.7 13.5 %all-gather.1 = bf16[4,1,2048]{2,1,0:T(2,128)(2,1)S(1)} all-gather(bf16[1,1,2048]{2,1,0:T(2,128)(2,1)S(1)} %bitcast.38), channel_id=1, replica_groups=mesh['ex'=4,'col'=4,'lay'=2] {'ex'}, dimensions={0}, use_global_device_ids=true | all-gather | bytes 20480 | tf_op jit(solution)/shard_map/all_gather | solution.py:54
  37.2 0.0 all-to-all-done
  37.2 0.1 reshape.103
  37.4 6.8 %all-gather = bf16[32,2,1,3584]{3,0,1,2:T(8,128)(2,1)S(1)} all-gather(bf16[32,2,1,896]{3,0,1,2:T(8,128)(2,1)S(1)} %bitcast.34), channel_id=2, replica_groups=mesh['ex'=4,'col'=4,'lay'=2] {'col'}, dimensions={3}, use_global_device_ids=true | all-gather | bytes 573440 | tf_op jit(solution)/shard_map/all_gather | solution.py:37
  44.2 0.5 copy.41
  44.7 0.3 reshape.83
  45.0 0.5 convolution_bitcast_fusion
  45.4 0.4 convolution_convert_fusion
  45.9 0.0 copy-start
  45.9 0.1 fusion.20
  46.1 6.6 %all-reduce = f32[32,4]{0,1:T(4,128)S(1)} all-reduce(f32[32,4]{0,1:T(4,128)S(1)} %fusion.20), channel_id=3, replica_groups=mesh['ex'=4,'col'=4,'lay'=2] {'col'}, use_global_device_ids=true, to_apply=%region_2.3.clone | all-reduce | flops 128 | bytes 1024
  52.7 1.2 %constant_dynamic-slice_fusion = f32[32,1]{0,1:T(1,128)} fusion(f32[32,4]{0,1:T(4,128)S(1)} %all-reduce, u32[]{:T(128)} %bitcast.9), kind=kLoop, calls=%fused_computation.38 | loop fusion | bytes 260
  53.9 0.0 copy-done
  (6 shorter events, 0.1 us)
Async XLA Ops:
  0.6 0.7 %copy-start.4 = (s32[1,64]{1,0:T(1,128)S(1)}, s32[1,64]{1,0:T(1,128)}, u32[]{:S(2)}) copy-start(s32[1,64]{1,0:T(1,128)} %param.8) | copy-start | bytes 772
  5.9 4.4 %copy-start.3 = (bf16[2,7,4]{1,2,0:T(4,128)(2,1)S(1)}, bf16[2,7,4]{1,2,0:T(4,128)(2,1)}, u32[]{:S(2)}) copy-start(bf16[2,7,4]{1,2,0:T(4,128)(2,1)} %param.10) | copy-start | bytes 340
  5.9 31.3 %all-to-all-start = ((bf16[2,2,14336]{2,1,0:T(2,128)(2,1)}), bf16[2,2,14336]{2,1,0:T(2,128)(2,1)S(1)}, u32[]{:S(2)}, u32[]{:S(2)}) async-start(bf16[2,2,14336]{2,1,0:T(2,128)(2,1)} %reshape.102), calls=%async_computation | async-start | bytes 229376 | tf_op jit(solution)/shard_map/all_to_all | solution.py:33
  15.9 0.7 %copy-start.2 = (s32[2,7,4]{1,2,0:T(4,128)S(1)}, s32[2,7,4]{1,2,0:T(4,128)}, u32[]{:S(2)}) copy-start(s32[2,7,4]{1,2,0:T(4,128)} %param.9) | copy-start | bytes 676
  22.3 1.3 %copy-start.1 = (bf16[1,2048]{1,0:T(2,128)(2,1)S(1)}, bf16[1,2048]{1,0:T(2,128)(2,1)}, u32[]{:S(2)}) copy-start(bf16[1,2048]{1,0:T(2,128)(2,1)} %param.11) | copy-start | bytes 12292
  22.4 0.7 %copy-start.5 = (u32[32]{0:T(128)S(1)}, u32[32]{0:T(128)}, u32[]{:S(2)}) copy-start(u32[32]{0:T(128)} %constant.65) | copy-start | bytes 388
  45.9 7.9 %copy-start = (bf16[4,8,16,128]{3,1,2,0:T(8,128)(2,1)}, bf16[4,8,16,128]{3,1,2,0:T(8,128)(2,1)S(1)}, u32[]{:S(2)}) copy-start(bf16[4,8,16,128]{3,1,2,0:T(8,128)(2,1)S(1)} %copy.51) | copy-start | bytes 393220
where the time goes:
time: 54.3 us; the launch traced here: 53.9 us
  blocking collectives  37.8 us (70%)
  local copies, waits for them, and re-layouts  6.38 us (12%)
  starting transfers between devices  4.37 us (8%)
  other arithmetic  3.53 us (7%)
  matrix products  1.03 us (2%)
  between operations  0.78 us (1%)
    all_gather x1, blocking collectives, local(): lax.all_gather(query_sketch, 'ex', axis=0, tiled=True)  13.5 us
    all_gather x1, blocking collectives, local(): lax.all_gather(owned, 'col', axis=2, tiled=True)  6.84 us
    unnamed x1, blocking collectives  6.58 us
    all_gather x1, blocking collectives, local(): lax.all_gather(sketch_index, 'col', axis=1, tiled=True)  5.43 us
    all_gather x1, blocking collectives, local(): lax.all_gather(sketch_scale, 'col', axis=1, tiled=True)  5.39 us
    all_to_all x1, starting transfers between devices, local(): lax.all_to_all(reordered, 'lay', split_axis=0, concat_axis=1, tiled=True)  4.37 us
    unnamed x20, local copies, waits for them, and re-layouts  4.15 us
    reduce_sum x1, other arithmetic, local(): jnp.sum(normalized.astype(jnp.float32) * upstream.astype(jnp.float32), ax...  1.84 us
  transfers between devices with their start and end apart: 1, of which 0 were waited for; matrix products, arithmetic and copies ran while one was open for 2% of the time, Pallas kernels for 0%

commit v1 on v0

--- a/solution.py
+++ b/solution.py
@@ -5,6 +5,27 @@
 from jax.sharding import PartitionSpec as P
 
 SKETCH = 8192
+
+
+def collect(value, axis, dim):
+    devices, mine, rows = (lax.axis_size(axis), lax.axis_index(axis), value.shape[dim])
+    upward = [(i, (i + 1) % devices) for i in range(devices)]
+    left = [(i, (i - 1) % devices) for i in range(devices)]
+    whole = jnp.zeros((*value.shape[:dim], devices * rows, *value.shape[dim + 1 :]), value.dtype)
+    whole = lax.dynamic_update_slice_in_dim(whole, value, mine * rows, axis=dim)
+    from_left = from_right = value
+    half = devices // 2
+    for step in range(1, half + 1):
+        from_left = lax.ppermute(from_left, axis, upward)
+        whole = lax.dynamic_update_slice_in_dim(
+            whole, from_left, (mine - step) % devices * rows, axis=dim
+        )
+        if step < devices - half:
+            from_right = lax.ppermute(from_right, axis, left)
+            whole = lax.dynamic_update_slice_in_dim(
+                whole, from_right, (mine + step) % devices * rows, axis=dim
+            )
+    return whole
 
 
 def hadamard_table():
@@ -49,10 +70,7 @@
     rotated = jnp.einsum("eoc,cd->eod", summed, hadamard_table(), precision=lax.Precision.HIGHEST)
     sketch = rotated.reshape(own_rows, -1).astype(jnp.bfloat16)
     partial_scores = jnp.einsum(
-        "ec,qc->eq",
-        sketch,
-        lax.all_gather(query_sketch, "ex", axis=0, tiled=True),
-        preferred_element_type=jnp.float32,
+        "ec,qc->eq", sketch, collect(query_sketch, "ex", 0), preferred_element_type=jnp.float32
     )
     scores = lax.psum_scatter(partial_scores, "col", scatter_dimension=1, tiled=True)
     return (sketch, scores)

time: 54.3 us -> 48.9 us (0.901)
  blocking collectives: 37.8 us -> 24 us
  starting transfers between devices: 4.37 us -> 8.75 us
  waiting for transfers between devices: 0.01 us -> 3.08 us
  local copies, waits for them, and re-layouts: 6.38 us -> 7.32 us
    all_gather x1 -> x0, blocking collectives: 13.5 us -> none  [local(): lax.all_gather(query_sketch, 'ex', axis=0, tiled=True)]
    ppermute x0 -> x3, starting transfers between devices: none -> 5.26 us  [the longest x2 3.16 us: collect(): from_left = lax.ppermute(from_left, axis, upward)]
    ppermute x0 -> x3, waiting for transfers between devices: none -> 3.08 us  [the longest x2 3.07 us: collect(): from_left = lax.ppermute(from_left, axis, upward)]
    all_to_all x1, starting transfers between devices: 4.37 us -> 3.49 us  [local(): lax.all_to_all(reordered, 'lay', split_axis=0, concat_axis=1, tiled=True)]
    unnamed x20, local copies, waits for them, and re-layouts: 4.15 us -> 4.82 us
  transfers between devices with their start and end apart: 1 -> 4, of which waited for: 0 -> 1; matrix products, arithmetic and copies ran while one was open for 2% -> 14% of each run, Pallas kernels for 0% -> 0%
where the time goes in v1:
time: 48.9 us; the launch traced here: 48.5 us
  blocking collectives  24 us (49%)
  starting transfers between devices  8.75 us (18%)
  local copies, waits for them, and re-layouts  7.32 us (15%)
  other arithmetic  3.46 us (7%)
  waiting for transfers between devices  3.08 us (6%)
  matrix products  1.03 us (2%)
  between operations  0.94 us (2%)
    all_gather x1, blocking collectives, local(): lax.all_gather(owned, 'col', axis=2, tiled=True)  7 us
    unnamed x1, blocking collectives  6.58 us
    all_gather x1, blocking collectives, local(): lax.all_gather(sketch_index, 'col', axis=1, tiled=True)  5.2 us
    all_gather x1, blocking collectives, local(): lax.all_gather(sketch_scale, 'col', axis=1, tiled=True)  5.18 us
    unnamed x20, local copies, waits for them, and re-layouts  4.82 us
    all_to_all x1, starting transfers between devices, local(): lax.all_to_all(reordered, 'lay', split_axis=0, concat_axis=1, tiled=True)  3.49 us
    ppermute x2, starting transfers between devices, collect(): from_left = lax.ppermute(from_left, axis, upward)  3.16 us
    ppermute x2, waiting for transfers between devices, collect(): from_left = lax.ppermute(from_left, axis, upward)  3.07 us
  transfers between devices with their start and end apart: 4, of which 1 were waited for; matrix products, arithmetic and copies ran while one was open for 14% of the time, Pallas kernels for 0%

profile of v1, /device:TPU:0, one launch (start us, length us, event | category | flops | bytes accessed | tf_op | source)
XLA Modules:
  0.0 48.5 jit_solution(7467702039455661082)
XLA Ops:
  0.6 0.0 copy-start.4
  0.6 3.1 %collective-permute-start = (bf16[1,2048]{1,0:T(2,128)(2,1)}, bf16[1,2048]{1,0:T(2,128)(2,1)S(1)}, u32[]{:S(2)}, u32[]{:S(2)}) collective-permute-start(bf16[1,2048]{1,0:T(2,128)(2,1)} %param.11), channel_id=1, source_target_pairs={{0,8},{8,16},{16,24},{24,0},{1,9},{9,17},{17,25},{25,1},{2,10},{10... | collective-permute-start | bytes 12296 | tf_op jit(solution)/shard_map/ppermute | solution.py:19
  3.7 2.1 %collective-permute-start.1 = (bf16[1,2048]{1,0:T(2,128)(2,1)}, bf16[1,2048]{1,0:T(2,128)(2,1)S(1)}, u32[]{:S(2)}, u32[]{:S(2)}) collective-permute-start(bf16[1,2048]{1,0:T(2,128)(2,1)} %param.11), channel_id=1, source_target_pairs={{0,24},{8,0},{16,8},{24,16},{1,25},{9,1},{17,9},{25,17},{2,26},{10... | collective-permute-start | bytes 12296 | tf_op jit(solution)/shard_map/ppermute | solution.py:24
  5.8 0.7 %fusion.20 = s32[64]{0:T(128)S(1)} fusion(s32[1,64]{1,0:T(1,128)} %param.8), kind=kLoop, calls=%fused_computation.34 | loop fusion | flops 192 | bytes 512 | tf_op jit(solution)/shard_map/jit(_take)/jit(_where)/select_n | solution.py:53
  6.5 0.0 copy-done.4
  6.5 1.8 %multiply_reduce_fusion = bf16[64,896]{1,0:T(8,128)(2,1)S(1)} fusion(bf16[64,1,4,896]{3,2,1,0:T(4,128)(2,1)} %param.7, bf16[64,1,4,896]{3,2,1,0:T(4,128)(2,1)} %param.6), kind=kLoop, calls=%fused_computation.3 | loop fusion | flops 860160 | bytes 1032192 | tf_op jit(solution)/shard_map/reduce_sum | solution.py:50
  8.4 0.7 %gather_fusion = bf16[64,896]{1,0:T(8,128)(2,1)S(1)} fusion(bf16[64,896]{1,0:T(8,128)(2,1)S(1)} %multiply_reduce_fusion, s32[1024]{0:T(1024)S(1)} %pad_clamp_fusion), kind=kCustom, calls=%fused_computation | custom fusion | bytes 229632 | tf_op jit(solution)/shard_map/jit(_take)/gather | solution.py:53
  9.1 0.1 bitcast_select_fusion
  9.2 0.5 %broadcast.83 = bf16[]{:T(256)} broadcast(bf16[]{:T(256)} %constant.134), dimensions={} | broadcast | bytes 4 | tf_op jit(solution)/shard_map/jit(_take)/select_n | solution.py:53
  9.7 0.7 %reduce.1 = bf16[64,896]{1,0:T(8,128)(2,1)S(1)} reduce(bf16[64,1,896]{2,0,1:T(8,128)(2,1)S(1)} %bitcast_select_fusion, bf16[]{:T(256)} %broadcast.83), dimensions={1}, to_apply=%copy.40.reduce_sub_computation | reduce | bytes 229378 | tf_op jit(solution)/shard_map/jit(_take)/select_n | solution.py:53
  10.4 0.7 %reshape.100 = bf16[2,2,14336]{2,1,0:T(2,128)(2,1)} reshape(bf16[64,896]{1,0:T(8,128)(2,1)S(1)} %reduce.1) | data formatting | bytes 229376
  11.0 0.0 copy-start.3
  11.0 3.5 %all-to-all-start = ((bf16[2,2,14336]{2,1,0:T(2,128)(2,1)}), bf16[2,2,14336]{2,1,0:T(2,128)(2,1)S(1)}, u32[]{:S(2)}, u32[]{:S(2)}) async-start(bf16[2,2,14336]{2,1,0:T(2,128)(2,1)} %reshape.100), calls=%async_computation | async-start | bytes 229376 | tf_op jit(solution)/shard_map/all_to_all | solution.py:54
  14.5 0.0 copy-done.3
  14.6 0.1 copy.36
  14.7 5.2 %all_gather.10 = bf16[2,28,4]{2,0,1:T(2,128)(2,1)S(1)} all-gather(bf16[2,7,4]{2,0,1:T(2,128)(2,1)S(1)} %copy.36), channel_id=1, replica_groups=mesh['ex'=4,'col'=4,'lay'=2] {'col'}, dimensions={1}, use_global_device_ids=true | all-gather | bytes 560 | tf_op jit(solution)/shard_map/all_gather | solution.py:60
  19.8 0.1 copy.37
  20.0 0.0 copy-start.2
  20.0 0.1 copy.38
  20.1 0.6 %copy-done.2 = s32[2,7,4]{1,2,0:T(4,128)S(1)} copy-done((s32[2,7,4]{1,2,0:T(4,128)S(1)}, s32[2,7,4]{1,2,0:T(4,128)}, u32[]{:S(2)}) %copy-start.2) | copy-done | bytes 248
  20.6 0.1 copy.34
  20.7 5.2 %all_gather.9 = s32[2,28,4]{2,0,1:T(2,128)S(1)} all-gather(s32[2,7,4]{2,0,1:T(2,128)S(1)} %copy.34), channel_id=1, replica_groups=mesh['ex'=4,'col'=4,'lay'=2] {'col'}, dimensions={1}, use_global_device_ids=true | all-gather | bytes 1120 | tf_op jit(solution)/shard_map/all_gather | solution.py:59
  25.9 0.2 select_reduce_fusion
  26.1 0.0 collective-permute-done
  26.2 0.1 collective-permute-start.2
  26.3 0.0 copy-start.1
  26.3 0.7 %copy-done.1 = bf16[1,2048]{1,0:T(2,128)(2,1)S(1)} copy-done((bf16[1,2048]{1,0:T(2,128)(2,1)S(1)}, bf16[1,2048]{1,0:T(2,128)(2,1)}, u32[]{:S(2)}) %copy-start.1) | copy-done | bytes 4120
  27.0 0.1 dynamic_update_slice.12
  27.1 0.0 copy-start.5
  27.1 0.6 %copy-done.5 = u32[32]{0:T(128)S(1)} copy-done((u32[32]{0:T(128)S(1)}, u32[32]{0:T(128)}, u32[]{:S(2)}) %copy-start.5) | copy-done | bytes 152
  27.8 0.7 %dynamic-slice = u32[1]{0:T(128)} dynamic-slice(u32[32]{0:T(128)S(1)} %copy-done.5, u32[]{:T(128)S(6)} %add.98), dynamic_slice_sizes={1} | dynamic-slice | bytes 12
  28.4 0.1 dynamic_update_slice.13
  28.5 0.0 collective-permute-done.1
  28.5 0.1 dynamic_update_slice.14
  28.6 3.1 %collective-permute-done.2 = bf16[1,2048]{1,0:T(2,128)(2,1)S(1)} collective-permute-done((bf16[1,2048]{1,0:T(2,128)(2,1)S(1)}, bf16[1,2048]{1,0:T(2,128)(2,1)S(1)}, u32[]{:S(2)}, u32[]{:S(2)}) %collective-permute-start.2) | collective-permute-done | bytes 4128 | tf_op jit(solution)/shard_map/ppermute | solution.py:19
  31.7 0.1 dynamic_update_slice.15
  31.7 0.0 all-to-all-done
  31.7 0.1 reshape.101
  31.9 7.0 %all-gather = bf16[32,2,1,3584]{3,0,1,2:T(8,128)(2,1)S(1)} all-gather(bf16[32,2,1,896]{3,0,1,2:T(8,128)(2,1)S(1)} %bitcast.31), channel_id=2, replica_groups=mesh['ex'=4,'col'=4,'lay'=2] {'col'}, dimensions={3}, use_global_device_ids=true | all-gather | bytes 573440 | tf_op jit(solution)/shard_map/all_gather | solution.py:58
  38.9 0.5 copy.41
  39.4 0.3 reshape.83
  39.7 0.5 convolution_bitcast_fusion
  40.1 0.4 convolution_convert_fusion
  40.6 0.0 copy-start
  40.6 0.1 fusion.30
  40.8 6.6 %all-reduce = f32[32,4]{0,1:T(4,128)S(1)} all-reduce(f32[32,4]{0,1:T(4,128)S(1)} %fusion.30), channel_id=3, replica_groups=mesh['ex'=4,'col'=4,'lay'=2] {'col'}, use_global_device_ids=true, to_apply=%region_2.3.clone | all-reduce | flops 128 | bytes 1024
  47.3 1.2 %constant_dynamic-slice_fusion = f32[32,1]{0,1:T(1,128)} fusion(f32[32,4]{0,1:T(4,128)S(1)} %all-reduce, u32[]{:T(128)} %bitcast.8), kind=kLoop, calls=%fused_computation.35 | loop fusion | bytes 260
  48.5 0.0 copy-done
  (7 shorter events, 0.1 us)
Async XLA Ops:
  0.6 5.9 %copy-start.4 = (s32[1,64]{1,0:T(1,128)S(1)}, s32[1,64]{1,0:T(1,128)}, u32[]{:S(2)}) copy-start(s32[1,64]{1,0:T(1,128)} %param.8) | copy-start | bytes 772
  0.6 25.5 %collective-permute-start = (bf16[1,2048]{1,0:T(2,128)(2,1)}, bf16[1,2048]{1,0:T(2,128)(2,1)S(1)}, u32[]{:S(2)}, u32[]{:S(2)}) collective-permute-start(bf16[1,2048]{1,0:T(2,128)(2,1)} %param.11), channel_id=1, source_target_pairs={{0,8},{8,16},{16,24},{24,0},{1,9},{9,17},{17,25},{25,1},{2,10},{10... | collective-permute-start | bytes 12296 | tf_op jit(solution)/shard_map/ppermute | solution.py:19
  3.7 24.7 %collective-permute-start.1 = (bf16[1,2048]{1,0:T(2,128)(2,1)}, bf16[1,2048]{1,0:T(2,128)(2,1)S(1)}, u32[]{:S(2)}, u32[]{:S(2)}) collective-permute-start(bf16[1,2048]{1,0:T(2,128)(2,1)} %param.11), channel_id=1, source_target_pairs={{0,24},{8,0},{16,8},{24,16},{1,25},{9,1},{17,9},{25,17},{2,26},{10... | collective-permute-start | bytes 12296 | tf_op jit(solution)/shard_map/ppermute | solution.py:24
  11.0 3.5 %copy-start.3 = (bf16[2,7,4]{1,2,0:T(4,128)(2,1)S(1)}, bf16[2,7,4]{1,2,0:T(4,128)(2,1)}, u32[]{:S(2)}) copy-start(bf16[2,7,4]{1,2,0:T(4,128)(2,1)} %param.10) | copy-start | bytes 340
  11.0 20.7 %all-to-all-start = ((bf16[2,2,14336]{2,1,0:T(2,128)(2,1)}), bf16[2,2,14336]{2,1,0:T(2,128)(2,1)S(1)}, u32[]{:S(2)}, u32[]{:S(2)}) async-start(bf16[2,2,14336]{2,1,0:T(2,128)(2,1)} %reshape.100), calls=%async_computation | async-start | bytes 229376 | tf_op jit(solution)/shard_map/all_to_all | solution.py:54
  20.0 0.7 %copy-start.2 = (s32[2,7,4]{1,2,0:T(4,128)S(1)}, s32[2,7,4]{1,2,0:T(4,128)}, u32[]{:S(2)}) copy-start(s32[2,7,4]{1,2,0:T(4,128)} %param.9) | copy-start | bytes 676
  26.2 5.5 %collective-permute-start.2 = (bf16[1,2048]{1,0:T(2,128)(2,1)S(1)}, bf16[1,2048]{1,0:T(2,128)(2,1)S(1)}, u32[]{:S(2)}, u32[]{:S(2)}) collective-permute-start(bf16[1,2048]{1,0:T(2,128)(2,1)S(1)} %collective-permute-done), channel_id=1, source_target_pairs={{0,8},{8,16},{16,24},{24,0},{1,9},{9,17},{17,25},{25,1},{2,10},{10... | collective-permute-start | bytes 12296 | tf_op jit(solution)/shard_map/ppermute | solution.py:19
  26.3 0.7 %copy-start.1 = (bf16[1,2048]{1,0:T(2,128)(2,1)S(1)}, bf16[1,2048]{1,0:T(2,128)(2,1)}, u32[]{:S(2)}) copy-start(bf16[1,2048]{1,0:T(2,128)(2,1)} %param.11) | copy-start | bytes 12292
  27.1 0.7 %copy-start.5 = (u32[32]{0:T(128)S(1)}, u32[32]{0:T(128)}, u32[]{:S(2)}) copy-start(u32[32]{0:T(128)} %constant.93) | copy-start | bytes 388
  40.6 7.9 %copy-start = (bf16[4,8,16,128]{3,1,2,0:T(8,128)(2,1)}, bf16[4,8,16,128]{3,1,2,0:T(8,128)(2,1)S(1)}, u32[]{:S(2)}) copy-start(bf16[4,8,16,128]{3,1,2,0:T(8,128)(2,1)S(1)} %copy.46) | copy-start | bytes 393220
